TPU v7x, 32 devices: a whole 2x2x4 slice. The times are simulated.
32 devices in a mesh: dp: 4 (over x, core), ctx: 8 (over z, y).
Axes of the slice: x: 2, y: 2, z: 4, core: 2. Of those that a mesh axis runs over, the one named last changes fastest.
Arguments:
- query: bfloat16 [4, 1024, 2048], P('dp', 'ctx'), may hold values from -6 to 6
- keys: bfloat16 [4, 1024, 2048], P('dp', 'ctx'), may hold values from -6 to 6
- values: bfloat16 [4, 1024, 2048], P('dp', 'ctx'), may hold values from -6 to 6
- cotangent: bfloat16 [4, 1024, 2048], P('dp', 'ctx'), may hold values from -6 to 6
- long_filter: bfloat16 [1024, 2048], P('ctx'), may hold values from -1.05 to 1.05, as said below
- short_weights: float32 [3, 3, 2048], replicated, may hold values from -3 to 3
- skip: float32 [2048], replicated, may hold values from -4 to 4
- lengths: int32 [4, 16], P('dp'), may hold values from 1 to 256, 1024 in all within a row
Outputs:
- gated: bfloat16 [4, 1024, 2048], P('dp', 'ctx')
- grad_query: bfloat16 [4, 1024, 2048], P('dp', 'ctx')
- grad_keys: bfloat16 [4, 1024, 2048], P('dp', 'ctx')
- grad_values: bfloat16 [4, 1024, 2048], P('dp', 'ctx')
- grad_filter: float32 [1024, 2048], P('ctx', 'dp')
- grad_short: float32 [3, 3, 2048], replicated
- grad_skip: float32 [2048], replicated
Inputs may be any that keep to these rules, and one draw needn't show every extreme that they name: Each row lists, in order, the lengths of the 16 documents packed into one sequence; they sum to 1024 and the longest is exactly 256. `long_filter`: one filter for every channel over the lags 0 .. 1023.
All inputs are finite; a program needn't handle non-finite values.
Results may differ from a plain program's by a relative error of at most 0.024.
Values may be sent and summed in bfloat16 or wider, within the bound.
No kernel may reach another device: no remote copies, remote signals or barrier semaphores. Data moves between devices by JAX's collectives and lax.ppermute only.
A program may use at most 192 MiB of HBM per device.

v0:
```python
import jax
import jax.numpy as jnp
from jax import lax
from jax.sharding import PartitionSpec as P


def shifted(x, axis, by):
    length = lax.axis_size(axis)
    pairs = [(i, i + by) for i in range(length) if 0 <= i + by < length]
    return lax.ppermute(x, axis, pairs)


def angles(time_idx, freq_idx, modulus, twist):
    turns = 2 * (time_idx * freq_idx % modulus) - twist * time_idx
    return jnp.pi * turns.astype(jnp.float32) / modulus


def table_halves(table):
    upper = lax.optimization_barrier(table.astype(jnp.bfloat16))
    lower = (table - upper.astype(jnp.float32)).astype(jnp.bfloat16)
    return (upper, lower)


def split_product(form, table, data):
    upper, lower = table_halves(table)
    if data.dtype == jnp.bfloat16:
        total = jnp.einsum(form, upper, data, preferred_element_type=jnp.float32)
        return total + jnp.einsum(form, lower, data, preferred_element_type=jnp.float32)
    data_upper = lax.optimization_barrier(data.astype(jnp.bfloat16))
    data_lower = (data - data_upper.astype(jnp.float32)).astype(jnp.bfloat16)
    total = jnp.einsum(form, upper, data_upper, preferred_element_type=jnp.float32)
    total = total + jnp.einsum(form, lower, data_upper, preferred_element_type=jnp.float32)
    return total + jnp.einsum(form, upper, data_lower, preferred_element_type=jnp.float32)


def dft_block(rows, direction):
    steps = jnp.arange(rows, dtype=jnp.int32)
    phase = angles(steps[:, None], steps[None, :], rows, 0)
    cosine = jnp.cos(phase)
    sine = direction * jnp.sin(phase)
    upper = jnp.concatenate([cosine, sine], 1)
    lower = jnp.concatenate([-sine, cosine], 1)
    return jnp.concatenate([upper, lower], 0)


def to_columns(data):
    return lax.all_to_all(data, "ctx", split_axis=0, concat_axis=0, tiled=True)


def to_rows(data):
    return lax.all_to_all(data, "ctx", split_axis=0, concat_axis=0, tiled=True)


def forward_spectrum(columns, index):
    parts, block, chans = columns.shape
    rows = parts * block
    seq_len = rows * parts
    time_p = jnp.arange(parts, dtype=jnp.int32)[None, :]
    freq_k = jnp.arange(parts, dtype=jnp.int32)[:, None]
    tables = []
    for twist in range(2):
        phase = angles(time_p, freq_k, parts, twist)
        tables.append(jnp.cos(phase))
        tables.append(-jnp.sin(phase))
    table = jnp.stack(tables).reshape(4 * parts, parts)
    flat = columns.reshape(parts, block * chans)
    partial_value = split_product("kp,pm->km", table, flat)
    partial_value = partial_value.reshape(2, 2, parts, block, chans)
    local_m = index * block + jnp.arange(block, dtype=jnp.int32)
    twiddled = []
    for twist in range(2):
        phase = angles(local_m[None, :], freq_k, seq_len, twist)[:, :, None]
        cosine = jnp.cos(phase)
        sine = jnp.sin(phase)
        real_part = partial_value[twist, 0]
        imag_part = partial_value[twist, 1]
        twiddled.append(real_part * cosine + imag_part * sine)
        twiddled.append(imag_part * cosine - real_part * sine)
    moved = lax.all_to_all(jnp.stack(twiddled), "ctx", split_axis=1, concat_axis=2, tiled=True)
    data = moved.reshape(2, 2 * rows, chans)
    spectrum = split_product("ab,sbc->sac", dft_block(rows, 1.0), data)
    return spectrum.reshape(2, 2, rows, chans)


def inverse_spectrum(spectrum, index, parts):
    rows, chans = (spectrum.shape[2], spectrum.shape[3])
    block = rows // parts
    seq_len = rows * parts
    data = spectrum.reshape(2, 2 * rows, chans)
    back = split_product("ab,sbc->sac", dft_block(rows, -1.0), data).reshape(2, 2, rows, chans)
    local_m = jnp.arange(rows, dtype=jnp.int32)[:, None]
    twisted = []
    for twist in range(2):
        phase = angles(local_m, index, seq_len, twist)
        cosine = jnp.cos(phase)
        sine = jnp.sin(phase)
        real_part = back[twist, 0]
        imag_part = back[twist, 1]
        twisted.append(real_part * cosine - imag_part * sine)
        twisted.append(imag_part * cosine + real_part * sine)
    stacked = jnp.stack(twisted).reshape(4, parts, block, chans)
    moved = (
        lax.all_to_all(stacked.astype(jnp.bfloat16), "ctx", split_axis=1, concat_axis=2, tiled=True)
        .astype(stacked.dtype)
        .reshape(4 * parts, block * chans)
    )
    time_p = jnp.arange(parts, dtype=jnp.int32)[:, None]
    freq_k = jnp.arange(parts, dtype=jnp.int32)[None, :]
    pieces = []
    for twist in range(2):
        phase = angles(time_p, freq_k, parts, twist)
        pieces.append(jnp.cos(phase))
        pieces.append(-jnp.sin(phase))
    table = jnp.stack(pieces, axis=1).reshape(parts, 4 * parts) / (2.0 * seq_len)
    result = split_product("kp,pm->km", table, moved)
    return result.reshape(parts, block, chans)


def spectrum_of(signal, index, parts):
    rows, channels = signal.shape
    columns = to_columns(signal).reshape(parts, rows // parts, channels)
    return forward_spectrum(columns, index)


def signal_of(spectrum, index, parts):
    rows, channels = (spectrum.shape[2], spectrum.shape[3])
    return to_rows(inverse_spectrum(spectrum, index, parts).reshape(rows, channels))


def complex_product(left_re, left_im, right_re, right_im, conjugate_left):
    if conjugate_left:
        return (left_re * right_re + left_im * right_im, left_re * right_im - left_im * right_re)
    return (left_re * right_re - left_im * right_im, left_re * right_im + left_im * right_re)


def spectral_product(first, second, conjugate_left):
    twists = []
    for twist in range(2):
        twists.append(
            jnp.stack(
                complex_product(
                    first[twist, 0],
                    first[twist, 1],
                    second[twist, 0],
                    second[twist, 1],
                    conjugate_left,
                )
            )
        )
    return jnp.stack(twists)


def short_forward(padded, weights, valid):
    count = weights.shape[0]
    rows = padded.shape[0] - count + 1
    wide = padded.astype(jnp.float32)
    summed = weights[0] * wide[count - 1 :]
    for offset in range(1, count):
        begin = count - 1 - offset
        summed = summed + jnp.where(
            valid[offset][:, None], weights[offset] * wide[begin : begin + rows], 0.0
        )
    return summed


def short_backward(padded, grad_short, after, weights, valid, valid_after):
    count = weights.shape[0]
    rows = grad_short.shape[0]
    wide = padded.astype(jnp.float32)
    extended = jnp.concatenate([grad_short, after], 0)
    grad_source = weights[0] * grad_short
    weight_grads = [jnp.sum(wide[count - 1 :] * grad_short, axis=0)]
    for offset in range(1, count):
        later = jnp.where(
            valid_after[offset, offset : offset + rows][:, None],
            extended[offset : offset + rows],
            0.0,
        )
        grad_source = grad_source + weights[offset] * later
        masked = jnp.where(valid[offset][:, None], grad_short, 0.0)
        begin = count - 1 - offset
        weight_grads.append(jnp.sum(masked * wide[begin : begin + rows], axis=0))
    return (grad_source, jnp.stack(weight_grads))


def local(query, keys, values, cotangent, long_filter, short_weights, skip, lengths):
    parts = lax.axis_size("ctx")
    index = lax.axis_index("ctx")
    groups = lax.axis_size("dp")
    q_rows = query[0]
    k_rows = keys[0]
    v_rows = values[0]
    upstream = cotangent[0].astype(jnp.float32)
    rows, chans = q_rows.shape
    taps = short_weights.shape[1]
    seq_len = rows * parts
    doc_len = lengths[0]
    starts = jnp.cumsum(doc_len) - doc_len

    def valid_mask(where):
        begin = jnp.max(jnp.where(starts[None, :] <= where[:, None], starts[None, :], 0), axis=1)
        shifts = jnp.arange(taps, dtype=jnp.int32)[:, None]
        return where[None, :] - shifts >= begin[None, :]

    position = index * rows + jnp.arange(rows, dtype=jnp.int32)
    valid = valid_mask(position)
    valid_after = valid_mask(index * rows + jnp.arange(rows + taps - 1, dtype=jnp.int32))
    edge = rows - taps + 1
    rim = shifted((q_rows[edge:], k_rows[edge:], v_rows[edge:]), "ctx", 1)
    padded_q = jnp.concatenate([rim[0], q_rows], 0)
    padded_k = jnp.concatenate([rim[1], k_rows], 0)
    padded_v = jnp.concatenate([rim[2], v_rows], 0)
    q_short = (
        short_forward(padded_q, short_weights[0], valid).astype(jnp.bfloat16).astype(jnp.float32)
    )
    k_short = (
        short_forward(padded_k, short_weights[1], valid).astype(jnp.bfloat16).astype(jnp.float32)
    )
    v_short = (
        short_forward(padded_v, short_weights[2], valid).astype(jnp.bfloat16).astype(jnp.float32)
    )
    mixed = (k_short * v_short).astype(jnp.bfloat16)
    grad_conv = (upstream * q_short).astype(jnp.bfloat16)
    mixed_wide = mixed.astype(jnp.float32)
    grad_wide = grad_conv.astype(jnp.float32)
    spectrum_f = spectrum_of(long_filter, index, parts)
    spectrum_x = spectrum_of(mixed, index, parts)
    spectrum_g = spectrum_of(grad_conv, index, parts)
    conv_spec = spectral_product(spectrum_x, spectrum_f, False)
    back_spec = spectral_product(spectrum_f, spectrum_g, True)
    cross_spec = spectral_product(spectrum_x, spectrum_g, True)
    conv_raw = signal_of(conv_spec, index, parts)
    back_raw = signal_of(back_spec, index, parts)
    lagged = signal_of(cross_spec, index, parts)
    filter_part = lax.psum_scatter(
        lagged.astype(jnp.bfloat16), "dp", scatter_dimension=1, tiled=True
    ).astype(jnp.float32)
    conv = conv_raw + skip * mixed_wide
    gated = (q_short * conv).astype(jnp.bfloat16)
    grad_qs = upstream * conv
    grad_mixed = back_raw + skip * grad_wide
    grad_ks = grad_mixed * v_short
    grad_vs = grad_mixed * k_short
    skip_grad = jnp.sum(grad_wide * mixed_wide, axis=0)
    head = taps - 1
    after = shifted((grad_qs[:head], grad_ks[:head], grad_vs[:head]), "ctx", -1)
    grad_q, short_q = short_backward(
        padded_q, grad_qs, after[0], short_weights[0], valid, valid_after
    )
    grad_k, short_k = short_backward(
        padded_k, grad_ks, after[1], short_weights[1], valid, valid_after
    )
    grad_v, short_v = short_backward(
        padded_v, grad_vs, after[2], short_weights[2], valid, valid_after
    )
    summed = lax.psum((jnp.stack([short_q, short_k, short_v]), skip_grad), ("dp", "ctx"))
    scale = 1.0 / (groups * seq_len)
    return (
        gated[None],
        grad_q.astype(jnp.bfloat16)[None],
        grad_k.astype(jnp.bfloat16)[None],
        grad_v.astype(jnp.bfloat16)[None],
        filter_part * scale,
        summed[0] * scale,
        summed[1] * scale,
    )


def solution(mesh):
    in_specs = (
        P("dp", "ctx", None),
        P("dp", "ctx", None),
        P("dp", "ctx", None),
        P("dp", "ctx", None),
        P("ctx", None),
        P(),
        P(),
        P("dp", None),
    )
    out_specs = (
        P("dp", "ctx", None),
        P("dp", "ctx", None),
        P("dp", "ctx", None),
        P("dp", "ctx", None),
        P("ctx", "dp"),
        P(),
        P(),
    )
    return jax.shard_map(local, mesh=mesh, in_specs=in_specs, out_specs=out_specs, check_vma=False)
```

profile of v0, /device:TPU:8, one launch (start us, length us, event | category | flops | bytes accessed | tf_op | source)
XLA Modules:
  0.0 839.3 jit_solution(11256855569213254024)
XLA Ops:
  8.8 3.4 collective-permute-start
  13.1 3.4 collective-permute-start.1
  17.3 3.4 collective-permute-start.2
  20.7 4.5 all-to-all-start.2
  31.7 3.6 fusion.25
  35.3 2.2 all-to-all-done.2
  37.6 4.9 all-to-all-start
  45.8 9.1 %all-to-all-done = bf16[8,16,2048]{2,1,0:T(8,128)(2,1)S(1)} async-done(((bf16[8,16,2048]{2,1,0:T(8,128)(2,1)}), bf16[8,16,2048]{2,1,0:T(8,128)(2,1)S(1)}, u32[]{:S(2)}, u32[]{:S(2)}) %all-to-all-start) | async-done | bytes 524320 | tf_op jit(solution)/shard_map/all_to_all | solution.py:47
  55.0 5.1 all-to-all-start.6
  61.7 2.1 fusion.110
  63.8 8.6 %all-to-all-done.6 = bf16[8,16,2048]{2,1,0:T(8,128)(2,1)S(1)} async-done(((bf16[8,16,2048]{2,1,0:T(8,128)(2,1)}), bf16[8,16,2048]{2,1,0:T(8,128)(2,1)S(1)}, u32[]{:S(2)}, u32[]{:S(2)}) %all-to-all-start.6) | async-done | bytes 524320 | tf_op jit(solution)/shard_map/all_to_all | solution.py:47
  76.2 5.5 multiply_add_fusion.1
  81.8 6.2 multiply_add_fusion
  88.0 2.3 pad_maximum_fusion.1
  90.3 5.9 all-to-all-start.3
  96.1 4.0 pad_maximum_fusion
  100.2 85.5 %all-to-all-done.3 = f32[4,8,16,2048]{3,2,0,1:T(8,128)} async-done(((f32[4,8,16,2048]{3,2,0,1:T(8,128)}), f32[4,8,16,2048]{3,2,0,1:T(8,128)}, u32[]{:S(2)}, u32[]{:S(2)}) %all-to-all-start.3) | async-done | bytes 4194336 | tf_op jit(solution)/shard_map/all_to_all | solution.py:79
  185.7 7.0 all-to-all-start.1
  192.7 3.6 pad_maximum_fusion.3
  196.2 86.5 %all-to-all-done.1 = f32[4,8,16,2048]{3,2,0,1:T(8,128)} async-done(((f32[4,8,16,2048]{3,2,0,1:T(8,128)}), f32[4,8,16,2048]{3,2,0,1:T(8,128)}, u32[]{:S(2)}, u32[]{:S(2)}) %all-to-all-start.1) | async-done | bytes 4194336 | tf_op jit(solution)/shard_map/all_to_all | solution.py:79
  282.7 7.0 all-to-all-start.7
  290.8 2.5 copy.113
  293.3 2.1 copy-done.8
  295.7 3.2 copy.108
  301.0 2.7 fusion.54
  303.6 2.8 fusion.120
  306.5 2.7 fusion.119
  309.2 2.8 fusion.51
  311.9 67.9 %all-to-all-done.7 = f32[4,8,16,2048]{3,2,0,1:T(8,128)} async-done(((f32[4,8,16,2048]{3,2,0,1:T(8,128)}), f32[4,8,16,2048]{3,2,0,1:T(8,128)}, u32[]{:S(2)}, u32[]{:S(2)}) %all-to-all-start.7) | async-done | bytes 4194336 | tf_op jit(solution)/shard_map/all_to_all | solution.py:79
  379.8 2.5 copy.120
  382.6 2.8 fusion.122
  385.4 2.9 fusion.57
  389.9 3.6 add_add_fusion.4
  393.5 4.6 add_add_fusion.5
  400.9 2.8 fusion.121
  403.6 4.8 add_add_fusion.2
  410.5 2.8 fusion.123
  413.3 2.7 fusion.45
  418.9 2.8 fusion.48
  422.4 3.0 add_add_fusion.3
  425.4 3.7 fusion.109
  436.5 2.4 subtract_convert_fusion.19
  438.9 2.4 subtract_convert_fusion.18
  442.9 6.6 all-to-all-start.4
  449.5 2.8 pad_maximum_fusion.11
  452.3 43.1 %all-to-all-done.4 = bf16[4,8,16,2048]{3,2,0,1:T(8,128)(2,1)S(1)} async-done(((bf16[4,8,16,2048]{3,2,0,1:T(8,128)(2,1)}), bf16[4,8,16,2048]{3,2,0,1:T(8,128)(2,1)S(1)}, u32[]{:S(2)}, u32[]{:S(2)}) %all-to-all-start.4) | async-done | bytes 2097184 | tf_op jit(solution)/shard_map/all_to_all | solution.py:103
  496.8 6.1 all-to-all-start.8
  502.9 2.8 pad_maximum_fusion.14
  505.7 43.2 %all-to-all-done.8 = bf16[4,8,16,2048]{3,2,0,1:T(8,128)(2,1)S(1)} async-done(((bf16[4,8,16,2048]{3,2,0,1:T(8,128)(2,1)}), bf16[4,8,16,2048]{3,2,0,1:T(8,128)(2,1)S(1)}, u32[]{:S(2)}, u32[]{:S(2)}) %all-to-all-start.8) | async-done | bytes 2097184 | tf_op jit(solution)/shard_map/all_to_all | solution.py:103
  550.2 6.1 all-to-all-start.10
  562.3 39.9 %all-to-all-done.10 = bf16[4,8,16,2048]{3,2,0,1:T(8,128)(2,1)S(1)} async-done(((bf16[4,8,16,2048]{3,2,0,1:T(8,128)(2,1)}), bf16[4,8,16,2048]{3,2,0,1:T(8,128)(2,1)S(1)}, u32[]{:S(2)}, u32[]{:S(2)}) %all-to-all-start.10) | async-done | bytes 2097184 | tf_op jit(solution)/shard_map/all_to_all | solution.py:103
  602.2 6.1 all-to-all-start.5
  614.2 17.7 %all-to-all-done.5 = f32[8,16,2048]{2,1,0:T(8,128)S(1)} async-done(((f32[8,16,2048]{2,1,0:T(8,128)}), f32[8,16,2048]{2,1,0:T(8,128)S(1)}, u32[]{:S(2)}, u32[]{:S(2)}) %all-to-all-start.5) | async-done | bytes 1048608 | tf_op jit(solution)/shard_map/all_to_all | solution.py:51
  632.9 6.0 all-to-all-start.9
  639.1 43.9 %psum.15 = f32[2048]{0:T(1024)S(1)} all-reduce(f32[2048]{0:T(1024)S(1)} %copy-done.61), channel_id=1, replica_groups=mesh['dp'=4,'ctx'=8] {'dp','ctx'}, use_global_device_ids=true, to_apply=%region_15.16 | all-reduce | flops 2048 | bytes 16384 | tf_op jit(solution)/shard_map/psum | solution.py:256
  687.2 3.1 multiply_reduce_fusion.8
  690.3 7.4 all-to-all-start.11
  697.7 3.9 multiply_reduce_fusion.2
  703.3 3.4 collective-permute-start.3
  707.3 2.2 all-to-all-done.11
  710.3 4.0 collective-permute-start.4
  714.3 2.7 collective-permute-start.5
  717.1 3.3 fusion.33
  722.6 105.8 %all-reduce.2.cloned.1.call-done = f32[3,3,2048]{2,1,0:T(4,128)} async-done(((f32[3,3,2048]{2,1,0:T(4,128)}), f32[3,3,2048]{2,1,0:T(4,128)}) %all-reduce.2.cloned.1.call-update) | async-done | bytes 73744 | tf_op jit(solution)/shard_map/psum | solution.py:256
  (248 shorter events, 68.3 us)
Async XLA Ops:
  8.0 22.0 %copy-start.41 = (bf16[1,128,2048]{2,1,0:T(8,128)(2,1)S(1)}, bf16[1,128,2048]{2,1,0:T(8,128)(2,1)}, u32[]{:S(2)}) copy-start(bf16[1,128,2048]{2,1,0:T(8,128)(2,1)} %param.9) | copy-start | bytes 1572868
  8.8 19.9 %collective-permute-start = (bf16[2,2048]{1,0:T(2,128)(2,1)S(1)}, bf16[2,2048]{1,0:T(2,128)(2,1)S(1)}, u32[]{:S(2)}, u32[]{:S(2)}) collective-permute-start(bf16[2,2048]{1,0:T(2,128)(2,1)S(1)} %slice_bitcast_fusion.2), channel_id=1, source_target_pairs={{0,1},{1,2},{2,3},{3,4},{4,5},{5,6},{6,7},{8,9},{9,10},{10,11},{11... | collective-permute-start | bytes 24584 | tf_op jit(solution)/shard_map/ppermute | solution.py:10
  13.1 16.9 %collective-permute-start.1 = (bf16[2,2048]{1,0:T(2,128)(2,1)S(1)}, bf16[2,2048]{1,0:T(2,128)(2,1)S(1)}, u32[]{:S(2)}, u32[]{:S(2)}) collective-permute-start(bf16[2,2048]{1,0:T(2,128)(2,1)S(1)} %slice_bitcast_fusion.1), channel_id=1, source_target_pairs={{0,1},{1,2},{2,3},{3,4},{4,5},{5,6},{6,7},{8,9},{9,10},{10,11},{11... | collective-permute-start | bytes 24584 | tf_op jit(solution)/shard_map/ppermute | solution.py:10
  17.3 12.9 %collective-permute-start.2 = (bf16[2,2048]{1,0:T(2,128)(2,1)S(1)}, bf16[2,2048]{1,0:T(2,128)(2,1)S(1)}, u32[]{:S(2)}, u32[]{:S(2)}) collective-permute-start(bf16[2,2048]{1,0:T(2,128)(2,1)S(1)} %slice_bitcast_fusion), channel_id=1, source_target_pairs={{0,1},{1,2},{2,3},{3,4},{4,5},{5,6},{6,7},{8,9},{9,10},{10,11},{11... | collective-permute-start | bytes 24584 | tf_op jit(solution)/shard_map/ppermute | solution.py:10
  20.7 9.5 %copy-start.42 = (bf16[1,128,2048]{2,1,0:T(8,128)(2,1)S(1)}, bf16[1,128,2048]{2,1,0:T(8,128)(2,1)}, u32[]{:S(2)}) copy-start(bf16[1,128,2048]{2,1,0:T(8,128)(2,1)} %param.10) | copy-start | bytes 1572868
  20.7 16.8 %all-to-all-start.2 = ((bf16[8,16,2048]{2,1,0:T(8,128)(2,1)}), bf16[8,16,2048]{2,1,0:T(8,128)(2,1)S(1)}, u32[]{:S(2)}, u32[]{:S(2)}) async-start(bf16[8,16,2048]{2,1,0:T(8,128)(2,1)} %bitcast.384), calls=%async_computation.2 | async-start | bytes 1048576 | tf_op jit(solution)/shard_map/all_to_all | solution.py:47
  28.7 3.0 copy-start.34
  37.6 17.4 %all-to-all-start = ((bf16[8,16,2048]{2,1,0:T(8,128)(2,1)}), bf16[8,16,2048]{2,1,0:T(8,128)(2,1)S(1)}, u32[]{:S(2)}, u32[]{:S(2)}) async-start(bf16[8,16,2048]{2,1,0:T(8,128)(2,1)} %bitcast.19), calls=%async_computation | async-start | bytes 1048576 | tf_op jit(solution)/shard_map/all_to_all | solution.py:47
  55.0 17.4 %all-to-all-start.6 = ((bf16[8,16,2048]{2,1,0:T(8,128)(2,1)}), bf16[8,16,2048]{2,1,0:T(8,128)(2,1)S(1)}, u32[]{:S(2)}, u32[]{:S(2)}) async-start(bf16[8,16,2048]{2,1,0:T(8,128)(2,1)} %bitcast.64), calls=%async_computation.6 | async-start | bytes 1048576 | tf_op jit(solution)/shard_map/all_to_all | solution.py:47
  74.1 2.1 copy-start.33
  76.2 5.5 copy-start.26
  76.2 5.5 copy-start.27
  90.3 5.9 copy-start.28
  90.3 5.9 copy-start.29
  90.3 95.4 %all-to-all-start.3 = ((f32[4,8,16,2048]{3,2,0,1:T(8,128)}), f32[4,8,16,2048]{3,2,0,1:T(8,128)}, u32[]{:S(2)}, u32[]{:S(2)}) async-start(f32[4,8,16,2048]{3,2,0,1:T(8,128)} %pad_maximum_fusion.1), calls=%async_computation.3 | async-start | bytes 8388608 | tf_op jit(solution)/shard_map/all_to_all | solution.py:79
  100.2 92.5 %copy-start.23 = (f32[1,8,16,2048]{3,2,0,1:T(8,128)S(1)}, f32[1,8,16,2048]{3,2,0,1:T(8,128)}, u32[]{:S(2)}) copy-start(f32[1,8,16,2048]{3,2,0,1:T(8,128)} %get-tuple-element.70) | copy-start | bytes 3145732
  100.2 92.5 %copy-start.31 = (f32[1,8,16,2048]{3,2,0,1:T(8,128)S(1)}, f32[1,8,16,2048]{3,2,0,1:T(8,128)}, u32[]{:S(2)}) copy-start(f32[1,8,16,2048]{3,2,0,1:T(8,128)} %get-tuple-element.71) | copy-start | bytes 3145732
  185.7 97.1 %all-to-all-start.1 = ((f32[4,8,16,2048]{3,2,0,1:T(8,128)}), f32[4,8,16,2048]{3,2,0,1:T(8,128)}, u32[]{:S(2)}, u32[]{:S(2)}) async-start(f32[4,8,16,2048]{3,2,0,1:T(8,128)} %pad_maximum_fusion), calls=%async_computation.1 | async-start | bytes 8388608 | tf_op jit(solution)/shard_map/all_to_all | solution.py:79
  282.7 97.1 %all-to-all-start.7 = ((f32[4,8,16,2048]{3,2,0,1:T(8,128)}), f32[4,8,16,2048]{3,2,0,1:T(8,128)}, u32[]{:S(2)}, u32[]{:S(2)}) async-start(f32[4,8,16,2048]{3,2,0,1:T(8,128)} %pad_maximum_fusion.3), calls=%async_computation.7 | async-start | bytes 8388608 | tf_op jit(solution)/shard_map/all_to_all | solution.py:79
  293.3 2.1 copy-start.8
  295.7 7.9 copy-start.10
  298.9 2.0 copy-start.6
  382.6 5.6 copy-start.16
  385.4 3.5 copy-start.9
  385.4 4.5 copy-start.11
  389.9 3.6 copy-start.7
  418.9 3.4 copy-start.12
  425.4 3.7 copy-start.13
  425.4 5.1 copy-start.14
  431.7 2.2 copy-start.15
  442.9 6.6 copy-start.39
  442.9 6.6 copy-start.40
  442.9 52.5 %all-to-all-start.4 = ((bf16[4,8,16,2048]{3,2,0,1:T(8,128)(2,1)}), bf16[4,8,16,2048]{3,2,0,1:T(8,128)(2,1)S(1)}, u32[]{:S(2)}, u32[]{:S(2)}) async-start(bf16[4,8,16,2048]{3,2,0,1:T(8,128)(2,1)} %pad_maximum_fusion.8), calls=%async_computation.4 | async-start | bytes 4194304 | tf_op jit(solution)/shard_map/all_to_all | solution.py:103
  452.3 50.6 %copy-start.37 = (bf16[1,8,16,2048]{3,2,0,1:T(8,128)(2,1)S(1)}, bf16[1,8,16,2048]{3,2,0,1:T(8,128)(2,1)}, u32[]{:S(2)}) copy-start(bf16[1,8,16,2048]{3,2,0,1:T(8,128)(2,1)} %get-tuple-element.61) | copy-start | bytes 1572868
  452.3 50.6 %copy-start.38 = (bf16[1,8,16,2048]{3,2,0,1:T(8,128)(2,1)S(1)}, bf16[1,8,16,2048]{3,2,0,1:T(8,128)(2,1)}, u32[]{:S(2)}) copy-start(bf16[1,8,16,2048]{3,2,0,1:T(8,128)(2,1)} %get-tuple-element.62) | copy-start | bytes 1572868
  496.8 52.1 %all-to-all-start.8 = ((bf16[4,8,16,2048]{3,2,0,1:T(8,128)(2,1)}), bf16[4,8,16,2048]{3,2,0,1:T(8,128)(2,1)S(1)}, u32[]{:S(2)}, u32[]{:S(2)}) async-start(bf16[4,8,16,2048]{3,2,0,1:T(8,128)(2,1)} %pad_maximum_fusion.11), calls=%async_computation.8 | async-start | bytes 4194304 | tf_op jit(solution)/shard_map/all_to_all | solution.py:103
  550.2 52.1 %all-to-all-start.10 = ((bf16[4,8,16,2048]{3,2,0,1:T(8,128)(2,1)}), bf16[4,8,16,2048]{3,2,0,1:T(8,128)(2,1)S(1)}, u32[]{:S(2)}, u32[]{:S(2)}) async-start(bf16[4,8,16,2048]{3,2,0,1:T(8,128)(2,1)} %pad_maximum_fusion.14), calls=%async_computation.10 | async-start | bytes 4194304 | tf_op jit(solution)/shard_map/all_to_all | solution.py:103
  602.2 29.7 %all-to-all-start.5 = ((f32[8,16,2048]{2,1,0:T(8,128)}), f32[8,16,2048]{2,1,0:T(8,128)S(1)}, u32[]{:S(2)}, u32[]{:S(2)}) async-start(f32[8,16,2048]{2,1,0:T(8,128)} %copy.115), calls=%async_computation.5 | async-start | bytes 2097152 | tf_op jit(solution)/shard_map/all_to_all | solution.py:51
  612.6 26.3 %copy-start.68 = (s32[16]{0:T(128)S(1)}, s32[16]{0:T(128)}, u32[]{:S(2)}) copy-start(s32[16]{0:T(128)} %copy-done.67) | copy-start | bytes 196
  612.6 26.5 %copy-start.61 = (f32[2048]{0:T(1024)S(1)}, f32[2048]{0:T(1024)}, u32[]{:S(2)}) copy-start(f32[2048]{0:T(1024)} %get-tuple-element.16) | copy-start | bytes 24580
  632.9 57.4 %all-to-all-start.9 = ((f32[8,16,2048]{2,1,0:T(8,128)}), f32[8,16,2048]{2,1,0:T(8,128)S(1)}, u32[]{:S(2)}, u32[]{:S(2)}) async-start(f32[8,16,2048]{2,1,0:T(8,128)} %copy.122), calls=%async_computation.9 | async-start | bytes 2097152 | tf_op jit(solution)/shard_map/all_to_all | solution.py:51
  685.2 2.0 copy-start.36
  685.2 2.0 copy-start.62
  685.2 2.0 copy-start.64
  685.2 2.0 copy-start.66
  687.2 10.5 %copy-start.1 = (f32[130,2048]{1,0:T(8,128)S(1)}, f32[130,2048]{1,0:T(8,128)}, u32[]{:S(2)}) copy-start(f32[130,2048]{1,0:T(8,128)} %copy-done) | copy-start | bytes 3194884
  687.2 10.5 %copy-start.3 = (f32[130,2048]{1,0:T(8,128)S(1)}, f32[130,2048]{1,0:T(8,128)}, u32[]{:S(2)}) copy-start(f32[130,2048]{1,0:T(8,128)} %copy-done.2) | copy-start | bytes 3194884
  690.3 7.4 copy-start.20
  690.3 19.1 %all-to-all-start.11 = ((bf16[8,16,2048]{2,1,0:T(8,128)(2,1)}), bf16[8,16,2048]{2,1,0:T(8,128)(2,1)}, u32[]{:S(2)}, u32[]{:S(2)}) async-start(bf16[8,16,2048]{2,1,0:T(8,128)(2,1)} %copy.124), calls=%async_computation.11 | async-start | bytes 1048576 | tf_op jit(solution)/shard_map/all_to_all | solution.py:51
  697.7 130.7 %all-reduce.2.cloned.1.call-start = ((), (), s32[]{:S(2)}) async-start(), calls=%async_computation.14 | async-start | bytes 196608 | tf_op jit(solution)/shard_map/psum | solution.py:256
  697.7 19.4 %copy-start.56 = (f32[1,1,2048]{2,1,0:T(1,128)S(1)}, f32[1,1,2048]{2,1,0:T(1,128)}, u32[]{:S(2)}) copy-start(f32[1,1,2048]{2,1,0:T(1,128)} %copy-done.55) | copy-start | bytes 24580
  697.7 19.4 %copy-start.58 = (f32[1,1,2048]{2,1,0:T(1,128)S(1)}, f32[1,1,2048]{2,1,0:T(1,128)}, u32[]{:S(2)}) copy-start(f32[1,1,2048]{2,1,0:T(1,128)} %copy-done.57) | copy-start | bytes 24580
  697.7 19.4 %copy-start.60 = (f32[1,1,2048]{2,1,0:T(1,128)S(1)}, f32[1,1,2048]{2,1,0:T(1,128)}, u32[]{:S(2)}) copy-start(f32[1,1,2048]{2,1,0:T(1,128)} %copy-done.59) | copy-start | bytes 24580
  701.6 18.9 %copy-start.19 = (f32[128,2048]{1,0:T(8,128)S(1)}, f32[128,2048]{1,0:T(8,128)}, u32[]{:S(2)}) copy-start(f32[128,2048]{1,0:T(8,128)} %get-tuple-element.88) | copy-start | bytes 3145732
  701.6 18.9 %copy-start.44 = (f32[1,1,2048]{2,1,0:T(1,128)S(1)}, f32[1,1,2048]{2,1,0:T(1,128)}, u32[]{:S(2)}) copy-start(f32[1,1,2048]{2,1,0:T(1,128)} %copy-done.43) | copy-start | bytes 24580
  701.6 18.9 %copy-start.46 = (f32[1,1,2048]{2,1,0:T(1,128)S(1)}, f32[1,1,2048]{2,1,0:T(1,128)}, u32[]{:S(2)}) copy-start(f32[1,1,2048]{2,1,0:T(1,128)} %copy-done.45) | copy-start | bytes 24580
  701.6 18.9 %copy-start.48 = (f32[1,1,2048]{2,1,0:T(1,128)S(1)}, f32[1,1,2048]{2,1,0:T(1,128)}, u32[]{:S(2)}) copy-start(f32[1,1,2048]{2,1,0:T(1,128)} %copy-done.47) | copy-start | bytes 24580
  701.6 18.9 %copy-start.50 = (f32[1,1,2048]{2,1,0:T(1,128)S(1)}, f32[1,1,2048]{2,1,0:T(1,128)}, u32[]{:S(2)}) copy-start(f32[1,1,2048]{2,1,0:T(1,128)} %copy-done.49) | copy-start | bytes 24580
  701.6 18.9 %copy-start.52 = (f32[1,1,2048]{2,1,0:T(1,128)S(1)}, f32[1,1,2048]{2,1,0:T(1,128)}, u32[]{:S(2)}) copy-start(f32[1,1,2048]{2,1,0:T(1,128)} %copy-done.51) | copy-start | bytes 24580
  701.6 18.9 %copy-start.54 = (f32[1,1,2048]{2,1,0:T(1,128)S(1)}, f32[1,1,2048]{2,1,0:T(1,128)}, u32[]{:S(2)}) copy-start(f32[1,1,2048]{2,1,0:T(1,128)} %copy-done.53) | copy-start | bytes 24580
  702.4 127.5 %reduce-scatter.2.cloned.1.call-start = ((), (), s32[]{:S(2)}) async-start(), calls=%async_computation.13 | async-start | bytes 655360 | tf_op jit(solution)/shard_map/reduce_scatter | solution.py:235
  703.3 13.7 %collective-permute-start.3 = (f32[2,2048]{1,0:T(2,128)S(1)}, f32[2,2048]{1,0:T(2,128)S(1)}, u32[]{:S(2)}, u32[]{:S(2)}) collective-permute-start(f32[2,2048]{1,0:T(2,128)S(1)} %slice.390), channel_id=1, source_target_pairs={{1,0},{2,1},{3,2},{4,3},{5,4},{6,5},{7,6},{9,8},{10,9},{11,10},{12... | collective-permute-start | bytes 49160 | tf_op jit(solution)/shard_map/ppermute | solution.py:10
  710.3 10.1 %collective-permute-start.4 = (f32[2,2048]{1,0:T(2,128)S(1)}, f32[2,2048]{1,0:T(2,128)S(1)}, u32[]{:S(2)}, u32[]{:S(2)}) collective-permute-start(f32[2,2048]{1,0:T(2,128)S(1)} %slice.406), channel_id=1, source_target_pairs={{1,0},{2,1},{3,2},{4,3},{5,4},{6,5},{7,6},{9,8},{10,9},{11,10},{12... | collective-permute-start | bytes 49160 | tf_op jit(solution)/shard_map/ppermute | solution.py:10
  714.3 6.1 collective-permute-start.5
  (25 other events, 39.2 us)
Sparse Core Ops, SparseCore 0:
  705.6 122.7 all-reduce.1
Sparse Core Ops, SparseCore 1:
  709.6 21.2 reduce-scatter.1
where the time goes:
time: 846 us; the launch traced here: 839 us
  waiting for transfers between devices  512 us (61%)
  starting transfers between devices  93 us (11%)
  other arithmetic  65.8 us (8%)
  matrix products  55.6 us (7%)
  local copies, waits for them, and re-layouts  52.2 us (6%)
  blocking collectives  43.9 us (5%)
  between operations  16.9 us (2%)
    all_to_all x3, waiting for transfers between devices, forward_spectrum(): lax.all_to_all(jnp.stack(twiddled), 'ctx', split_axis=1, concat_axis=2, t...  240 us
    all_to_all x3, waiting for transfers between devices, inverse_spectrum(): lax.all_to_all(stacked.astype(jnp.bfloat16), 'ctx', split_axis=1, concat_...  126 us
    psum x1, waiting for transfers between devices, local(): lax.psum((jnp.stack([short_q, short_k, short_v]), skip_grad), ('dp', 'ctx'))  106 us
    psum x1, blocking collectives, local(): lax.psum((jnp.stack([short_q, short_k, short_v]), skip_grad), ('dp', 'ctx'))  43.9 us
    unnamed x144, local copies, waits for them, and re-layouts  22.3 us
    ppermute x6, starting transfers between devices, shifted(): return lax.ppermute(x, axis, pairs)  20.3 us
    dot_general x9, matrix products, split_product(): jnp.einsum(form, upper, data_lower, preferred_element_type=jnp.float32)  20 us
    all_to_all x3, waiting for transfers between devices, to_columns(): return lax.all_to_all(data, 'ctx', split_axis=0, concat_axis=0, tiled=True)  20 us
  transfers between devices with their start and end apart: 20, of which 12 were waited for; matrix products, arithmetic and copies ran while one was open for 10% of the time, Pallas kernels for 0%

commit v1 on v0

--- a/solution.py
+++ b/solution.py
@@ -253,7 +253,8 @@
     grad_v, short_v = short_backward(
         padded_v, grad_vs, after[2], short_weights[2], valid, valid_after
     )
-    summed = lax.psum((jnp.stack([short_q, short_k, short_v]), skip_grad), ("dp", "ctx"))
+    half = lax.psum((jnp.stack([short_q, short_k, short_v]), skip_grad), "ctx")
+    summed = lax.psum(half, "dp")
     scale = 1.0 / (groups * seq_len)
     return (
         gated[None],

time: 846 us -> 817 us (0.966)
  blocking collectives: 43.9 us -> 24.7 us
    psum x1 -> x2, waiting for transfers between devices: 106 us -> 61.1 us  [the longest x1 41.5 us: local(): half = lax.psum((jnp.stack([short_q, short_k, short_v]), skip_grad), 'ctx')]
    reduce_scatter x1, waiting for transfers between devices: 0.01 us -> 22.7 us  [local(): lax.psum_scatter(lagged.astype(jnp.bfloat16), 'dp', scatter_dimension=1,...]
    psum x1 -> x2, blocking collectives: 43.9 us -> 24.7 us  [the longest x1 18.9 us: local(): half = lax.psum((jnp.stack([short_q, short_k, short_v]), skip_grad), 'ctx')]
    all_to_all x3, waiting for transfers between devices: 19.9 us -> 34 us  [to_rows(): return lax.all_to_all(data, 'ctx', split_axis=0, concat_axis=0, tiled=True)]
  transfers between devices with their start and end apart: 20 -> 21, of which waited for: 12 -> 14; matrix products, arithmetic and copies ran while one was open for 10% -> 10% of each run, Pallas kernels for 0% -> 0%
where the time goes in v1:
time: 817 us; the launch traced here: 809 us
  waiting for transfers between devices  504 us (62%)
  starting transfers between devices  91.4 us (11%)
  other arithmetic  65.9 us (8%)
  matrix products  55.5 us (7%)
  local copies, waits for them, and re-layouts  52 us (6%)
  blocking collectives  24.7 us (3%)
  between operations  15.2 us (2%)
    all_to_all x3, waiting for transfers between devices, forward_spectrum(): lax.all_to_all(jnp.stack(twiddled), 'ctx', split_axis=1, concat_axis=2, t...  240 us
    all_to_all x3, waiting for transfers between devices, inverse_spectrum(): lax.all_to_all(stacked.astype(jnp.bfloat16), 'ctx', split_axis=1, concat_...  126 us
    psum x1, waiting for transfers between devices, local(): half = lax.psum((jnp.stack([short_q, short_k, short_v]), skip_grad), 'ctx')  41.5 us
    all_to_all x3, waiting for transfers between devices, to_rows(): return lax.all_to_all(data, 'ctx', split_axis=0, concat_axis=0, tiled=True)  34 us
    reduce_scatter x1, waiting for transfers between devices, local(): lax.psum_scatter(lagged.astype(jnp.bfloat16), 'dp', scatter_dimension=1,...  22.7 us
    unnamed x144, local copies, waits for them, and re-layouts  22.2 us
    all_to_all x3, waiting for transfers between devices, to_columns(): return lax.all_to_all(data, 'ctx', split_axis=0, concat_axis=0, tiled=True)  20.1 us
    dot_general x9, matrix products, split_product(): jnp.einsum(form, upper, data_lower, preferred_element_type=jnp.float32)  20 us
  transfers between devices with their start and end apart: 21, of which 14 were waited for; matrix products, arithmetic and copies ran while one was open for 10% of the time, Pallas kernels for 0%

profile of v1, /device:TPU:8, one launch (start us, length us, event | category | flops | bytes accessed | tf_op | source)
XLA Modules:
  0.0 808.9 jit_solution(11520513715500787769)
XLA Ops:
  8.0 3.4 collective-permute-start
  12.2 3.4 collective-permute-start.1
  16.4 3.4 collective-permute-start.2
  19.9 4.5 all-to-all-start.2
  30.8 3.6 fusion.25
  34.4 2.3 all-to-all-done.2
  36.7 4.9 all-to-all-start
  45.0 9.1 %all-to-all-done = bf16[8,16,2048]{2,1,0:T(8,128)(2,1)S(1)} async-done(((bf16[8,16,2048]{2,1,0:T(8,128)(2,1)}), bf16[8,16,2048]{2,1,0:T(8,128)(2,1)S(1)}, u32[]{:S(2)}, u32[]{:S(2)}) %all-to-all-start) | async-done | bytes 524320 | tf_op jit(solution)/shard_map/all_to_all | solution.py:47
  54.1 5.1 all-to-all-start.6
  63.0 8.6 %all-to-all-done.6 = bf16[8,16,2048]{2,1,0:T(8,128)(2,1)S(1)} async-done(((bf16[8,16,2048]{2,1,0:T(8,128)(2,1)}), bf16[8,16,2048]{2,1,0:T(8,128)(2,1)S(1)}, u32[]{:S(2)}, u32[]{:S(2)}) %all-to-all-start.6) | async-done | bytes 524320 | tf_op jit(solution)/shard_map/all_to_all | solution.py:47
  75.4 5.5 multiply_add_fusion.1
  80.9 6.2 multiply_add_fusion
  89.5 5.9 all-to-all-start.3
  95.3 4.0 pad_maximum_fusion
  99.4 85.5 %all-to-all-done.3 = f32[4,8,16,2048]{3,2,0,1:T(8,128)} async-done(((f32[4,8,16,2048]{3,2,0,1:T(8,128)}), f32[4,8,16,2048]{3,2,0,1:T(8,128)}, u32[]{:S(2)}, u32[]{:S(2)}) %all-to-all-start.3) | async-done | bytes 4194336 | tf_op jit(solution)/shard_map/all_to_all | solution.py:79
  184.9 7.0 all-to-all-start.1
  191.9 3.6 pad_maximum_fusion.3
  195.4 86.5 %all-to-all-done.1 = f32[4,8,16,2048]{3,2,0,1:T(8,128)} async-done(((f32[4,8,16,2048]{3,2,0,1:T(8,128)}), f32[4,8,16,2048]{3,2,0,1:T(8,128)}, u32[]{:S(2)}, u32[]{:S(2)}) %all-to-all-start.1) | async-done | bytes 4194336 | tf_op jit(solution)/shard_map/all_to_all | solution.py:79
  281.9 7.0 all-to-all-start.7
  290.0 2.5 copy.113
  294.9 3.2 copy.108
  300.1 2.7 fusion.54
  302.8 2.8 fusion.120
  305.6 2.7 fusion.119
  308.4 2.7 fusion.51
  311.1 68.0 %all-to-all-done.7 = f32[4,8,16,2048]{3,2,0,1:T(8,128)} async-done(((f32[4,8,16,2048]{3,2,0,1:T(8,128)}), f32[4,8,16,2048]{3,2,0,1:T(8,128)}, u32[]{:S(2)}, u32[]{:S(2)}) %all-to-all-start.7) | async-done | bytes 4194336 | tf_op jit(solution)/shard_map/all_to_all | solution.py:79
  379.1 2.5 copy.120
  381.8 2.8 fusion.122
  384.6 2.9 fusion.57
  389.1 3.6 add_add_fusion.4
  392.7 4.6 add_add_fusion.5
  400.1 2.7 fusion.121
  402.8 4.8 add_add_fusion.2
  409.7 2.8 fusion.123
  412.5 2.8 fusion.45
  418.1 2.7 fusion.48
  421.5 3.0 add_add_fusion.3
  424.6 3.7 fusion.109
  435.7 2.4 subtract_convert_fusion.19
  438.1 2.4 subtract_convert_fusion.18
  442.1 6.6 all-to-all-start.4
  448.7 2.8 pad_maximum_fusion.11
  451.5 43.1 %all-to-all-done.4 = bf16[4,8,16,2048]{3,2,0,1:T(8,128)(2,1)S(1)} async-done(((bf16[4,8,16,2048]{3,2,0,1:T(8,128)(2,1)}), bf16[4,8,16,2048]{3,2,0,1:T(8,128)(2,1)S(1)}, u32[]{:S(2)}, u32[]{:S(2)}) %all-to-all-start.4) | async-done | bytes 2097184 | tf_op jit(solution)/shard_map/all_to_all | solution.py:103
  496.0 6.1 all-to-all-start.8
  502.1 2.8 pad_maximum_fusion.14
  504.9 43.1 %all-to-all-done.8 = bf16[4,8,16,2048]{3,2,0,1:T(8,128)(2,1)S(1)} async-done(((bf16[4,8,16,2048]{3,2,0,1:T(8,128)(2,1)}), bf16[4,8,16,2048]{3,2,0,1:T(8,128)(2,1)S(1)}, u32[]{:S(2)}, u32[]{:S(2)}) %all-to-all-start.8) | async-done | bytes 2097184 | tf_op jit(solution)/shard_map/all_to_all | solution.py:103
  549.4 6.1 all-to-all-start.10
  561.5 39.9 %all-to-all-done.10 = bf16[4,8,16,2048]{3,2,0,1:T(8,128)(2,1)S(1)} async-done(((bf16[4,8,16,2048]{3,2,0,1:T(8,128)(2,1)}), bf16[4,8,16,2048]{3,2,0,1:T(8,128)(2,1)S(1)}, u32[]{:S(2)}, u32[]{:S(2)}) %all-to-all-start.10) | async-done | bytes 2097184 | tf_op jit(solution)/shard_map/all_to_all | solution.py:103
  601.4 6.1 all-to-all-start.5
  613.3 17.8 %all-to-all-done.5 = f32[8,16,2048]{2,1,0:T(8,128)S(1)} async-done(((f32[8,16,2048]{2,1,0:T(8,128)}), f32[8,16,2048]{2,1,0:T(8,128)S(1)}, u32[]{:S(2)}, u32[]{:S(2)}) %all-to-all-start.5) | async-done | bytes 1048608 | tf_op jit(solution)/shard_map/all_to_all | solution.py:51
  632.1 6.0 all-to-all-start.9
  642.4 3.0 multiply_reduce_fusion.8
  645.4 16.2 %all-to-all-done.9 = f32[8,16,2048]{2,1,0:T(8,128)S(1)} async-done(((f32[8,16,2048]{2,1,0:T(8,128)}), f32[8,16,2048]{2,1,0:T(8,128)S(1)}, u32[]{:S(2)}, u32[]{:S(2)}) %all-to-all-start.9) | async-done | bytes 1048608 | tf_op jit(solution)/shard_map/all_to_all | solution.py:51
  661.6 6.4 all-to-all-start.11
  668.4 3.8 multiply_reduce_fusion.2
  673.2 18.9 %psum.30 = f32[2048]{0:T(1024)S(1)} all-reduce(f32[2048]{0:T(1024)S(1)} %copy-done.61), channel_id=1, replica_groups=mesh['dp'=4,'ctx'=8] {'ctx'}, use_global_device_ids=true, to_apply=%region_16.17 | all-reduce | flops 2048 | bytes 16384 | tf_op jit(solution)/shard_map/psum | solution.py:256
  692.1 5.8 psum.31
  698.7 2.6 collective-permute-start.3
  701.3 41.5 %all-reduce.3.cloned.1.call-done = f32[3,3,2048]{2,1,0:T(4,128)} async-done(((f32[3,3,2048]{2,1,0:T(4,128)}), f32[3,3,2048]{2,1,0:T(4,128)}) %all-reduce.3.cloned.1.call-update) | async-done | bytes 73744 | tf_op jit(solution)/shard_map/psum | solution.py:256
  744.4 3.4 collective-permute-start.4
  747.8 3.1 collective-permute-start.5
  751.0 3.4 fusion.33
  756.5 19.7 %all-reduce.5.cloned.1.call-done = f32[3,3,2048]{2,1,0:T(4,128)} async-done(((f32[3,3,2048]{2,1,0:T(4,128)}), f32[3,3,2048]{2,1,0:T(4,128)}) %all-reduce.5.cloned.1.call-update) | async-done | bytes 73744 | tf_op jit(solution)/shard_map/psum | solution.py:257
  777.7 22.7 %reduce-scatter.2.cloned.1.call-done = bf16[128,512]{1,0:T(8,128)(2,1)} async-done(((bf16[128,2048]{1,0:T(8,128)(2,1)}), bf16[128,512]{1,0:T(8,128)(2,1)}) %reduce-scatter.2.cloned.1.call-update) | async-done | bytes 131088 | tf_op jit(solution)/shard_map/reduce_scatter | solution.py:235
  (252 shorter events, 74.9 us)
Async XLA Ops:
  7.2 21.9 %copy-start.41 = (bf16[1,128,2048]{2,1,0:T(8,128)(2,1)S(1)}, bf16[1,128,2048]{2,1,0:T(8,128)(2,1)}, u32[]{:S(2)}) copy-start(bf16[1,128,2048]{2,1,0:T(8,128)(2,1)} %param.9) | copy-start | bytes 1572868
  8.0 19.8 %collective-permute-start = (bf16[2,2048]{1,0:T(2,128)(2,1)S(1)}, bf16[2,2048]{1,0:T(2,128)(2,1)S(1)}, u32[]{:S(2)}, u32[]{:S(2)}) collective-permute-start(bf16[2,2048]{1,0:T(2,128)(2,1)S(1)} %slice_bitcast_fusion.2), channel_id=1, source_target_pairs={{0,1},{1,2},{2,3},{3,4},{4,5},{5,6},{6,7},{8,9},{9,10},{10,11},{11... | collective-permute-start | bytes 24584 | tf_op jit(solution)/shard_map/ppermute | solution.py:10
  12.2 16.9 %collective-permute-start.1 = (bf16[2,2048]{1,0:T(2,128)(2,1)S(1)}, bf16[2,2048]{1,0:T(2,128)(2,1)S(1)}, u32[]{:S(2)}, u32[]{:S(2)}) collective-permute-start(bf16[2,2048]{1,0:T(2,128)(2,1)S(1)} %slice_bitcast_fusion.1), channel_id=1, source_target_pairs={{0,1},{1,2},{2,3},{3,4},{4,5},{5,6},{6,7},{8,9},{9,10},{10,11},{11... | collective-permute-start | bytes 24584 | tf_op jit(solution)/shard_map/ppermute | solution.py:10
  16.4 12.8 %collective-permute-start.2 = (bf16[2,2048]{1,0:T(2,128)(2,1)S(1)}, bf16[2,2048]{1,0:T(2,128)(2,1)S(1)}, u32[]{:S(2)}, u32[]{:S(2)}) collective-permute-start(bf16[2,2048]{1,0:T(2,128)(2,1)S(1)} %slice_bitcast_fusion), channel_id=1, source_target_pairs={{0,1},{1,2},{2,3},{3,4},{4,5},{5,6},{6,7},{8,9},{9,10},{10,11},{11... | collective-permute-start | bytes 24584 | tf_op jit(solution)/shard_map/ppermute | solution.py:10
  19.9 9.4 %copy-start.42 = (bf16[1,128,2048]{2,1,0:T(8,128)(2,1)S(1)}, bf16[1,128,2048]{2,1,0:T(8,128)(2,1)}, u32[]{:S(2)}) copy-start(bf16[1,128,2048]{2,1,0:T(8,128)(2,1)} %param.10) | copy-start | bytes 1572868
  19.9 16.8 %all-to-all-start.2 = ((bf16[8,16,2048]{2,1,0:T(8,128)(2,1)}), bf16[8,16,2048]{2,1,0:T(8,128)(2,1)S(1)}, u32[]{:S(2)}, u32[]{:S(2)}) async-start(bf16[8,16,2048]{2,1,0:T(8,128)(2,1)} %bitcast.384), calls=%async_computation.2 | async-start | bytes 1048576 | tf_op jit(solution)/shard_map/all_to_all | solution.py:47
  27.8 3.0 copy-start.34
  36.7 17.4 %all-to-all-start = ((bf16[8,16,2048]{2,1,0:T(8,128)(2,1)}), bf16[8,16,2048]{2,1,0:T(8,128)(2,1)S(1)}, u32[]{:S(2)}, u32[]{:S(2)}) async-start(bf16[8,16,2048]{2,1,0:T(8,128)(2,1)} %bitcast.19), calls=%async_computation | async-start | bytes 1048576 | tf_op jit(solution)/shard_map/all_to_all | solution.py:47
  54.1 17.4 %all-to-all-start.6 = ((bf16[8,16,2048]{2,1,0:T(8,128)(2,1)}), bf16[8,16,2048]{2,1,0:T(8,128)(2,1)S(1)}, u32[]{:S(2)}, u32[]{:S(2)}) async-start(bf16[8,16,2048]{2,1,0:T(8,128)(2,1)} %bitcast.64), calls=%async_computation.6 | async-start | bytes 1048576 | tf_op jit(solution)/shard_map/all_to_all | solution.py:47
  73.3 2.1 copy-start.33
  75.4 5.5 copy-start.26
  75.4 5.5 copy-start.27
  89.5 5.9 copy-start.28
  89.5 5.9 copy-start.29
  89.5 95.4 %all-to-all-start.3 = ((f32[4,8,16,2048]{3,2,0,1:T(8,128)}), f32[4,8,16,2048]{3,2,0,1:T(8,128)}, u32[]{:S(2)}, u32[]{:S(2)}) async-start(f32[4,8,16,2048]{3,2,0,1:T(8,128)} %pad_maximum_fusion.1), calls=%async_computation.3 | async-start | bytes 8388608 | tf_op jit(solution)/shard_map/all_to_all | solution.py:79
  99.4 92.5 %copy-start.23 = (f32[1,8,16,2048]{3,2,0,1:T(8,128)S(1)}, f32[1,8,16,2048]{3,2,0,1:T(8,128)}, u32[]{:S(2)}) copy-start(f32[1,8,16,2048]{3,2,0,1:T(8,128)} %get-tuple-element.70) | copy-start | bytes 3145732
  99.4 92.5 %copy-start.31 = (f32[1,8,16,2048]{3,2,0,1:T(8,128)S(1)}, f32[1,8,16,2048]{3,2,0,1:T(8,128)}, u32[]{:S(2)}) copy-start(f32[1,8,16,2048]{3,2,0,1:T(8,128)} %get-tuple-element.71) | copy-start | bytes 3145732
  184.9 97.1 %all-to-all-start.1 = ((f32[4,8,16,2048]{3,2,0,1:T(8,128)}), f32[4,8,16,2048]{3,2,0,1:T(8,128)}, u32[]{:S(2)}, u32[]{:S(2)}) async-start(f32[4,8,16,2048]{3,2,0,1:T(8,128)} %pad_maximum_fusion), calls=%async_computation.1 | async-start | bytes 8388608 | tf_op jit(solution)/shard_map/all_to_all | solution.py:79
  281.9 97.1 %all-to-all-start.7 = ((f32[4,8,16,2048]{3,2,0,1:T(8,128)}), f32[4,8,16,2048]{3,2,0,1:T(8,128)}, u32[]{:S(2)}, u32[]{:S(2)}) async-start(f32[4,8,16,2048]{3,2,0,1:T(8,128)} %pad_maximum_fusion.3), calls=%async_computation.7 | async-start | bytes 8388608 | tf_op jit(solution)/shard_map/all_to_all | solution.py:79
  292.5 2.1 copy-start.8
  294.9 7.9 copy-start.10
  298.1 2.0 copy-start.6
  381.8 5.6 copy-start.16
  384.6 3.5 copy-start.9
  384.6 4.5 copy-start.11
  389.1 3.6 copy-start.7
  418.1 3.4 copy-start.12
  424.6 3.7 copy-start.13
  424.6 5.1 copy-start.14
  430.9 2.2 copy-start.15
  442.1 6.6 copy-start.39
  442.1 6.6 copy-start.40
  442.1 52.5 %all-to-all-start.4 = ((bf16[4,8,16,2048]{3,2,0,1:T(8,128)(2,1)}), bf16[4,8,16,2048]{3,2,0,1:T(8,128)(2,1)S(1)}, u32[]{:S(2)}, u32[]{:S(2)}) async-start(bf16[4,8,16,2048]{3,2,0,1:T(8,128)(2,1)} %pad_maximum_fusion.8), calls=%async_computation.4 | async-start | bytes 4194304 | tf_op jit(solution)/shard_map/all_to_all | solution.py:103
  451.5 50.6 %copy-start.37 = (bf16[1,8,16,2048]{3,2,0,1:T(8,128)(2,1)S(1)}, bf16[1,8,16,2048]{3,2,0,1:T(8,128)(2,1)}, u32[]{:S(2)}) copy-start(bf16[1,8,16,2048]{3,2,0,1:T(8,128)(2,1)} %get-tuple-element.61) | copy-start | bytes 1572868
  451.5 50.6 %copy-start.38 = (bf16[1,8,16,2048]{3,2,0,1:T(8,128)(2,1)S(1)}, bf16[1,8,16,2048]{3,2,0,1:T(8,128)(2,1)}, u32[]{:S(2)}) copy-start(bf16[1,8,16,2048]{3,2,0,1:T(8,128)(2,1)} %get-tuple-element.62) | copy-start | bytes 1572868
  496.0 52.1 %all-to-all-start.8 = ((bf16[4,8,16,2048]{3,2,0,1:T(8,128)(2,1)}), bf16[4,8,16,2048]{3,2,0,1:T(8,128)(2,1)S(1)}, u32[]{:S(2)}, u32[]{:S(2)}) async-start(bf16[4,8,16,2048]{3,2,0,1:T(8,128)(2,1)} %pad_maximum_fusion.11), calls=%async_computation.8 | async-start | bytes 4194304 | tf_op jit(solution)/shard_map/all_to_all | solution.py:103
  549.4 52.1 %all-to-all-start.10 = ((bf16[4,8,16,2048]{3,2,0,1:T(8,128)(2,1)}), bf16[4,8,16,2048]{3,2,0,1:T(8,128)(2,1)S(1)}, u32[]{:S(2)}, u32[]{:S(2)}) async-start(bf16[4,8,16,2048]{3,2,0,1:T(8,128)(2,1)} %pad_maximum_fusion.14), calls=%async_computation.10 | async-start | bytes 4194304 | tf_op jit(solution)/shard_map/all_to_all | solution.py:103
  601.4 29.7 %all-to-all-start.5 = ((f32[8,16,2048]{2,1,0:T(8,128)}), f32[8,16,2048]{2,1,0:T(8,128)S(1)}, u32[]{:S(2)}, u32[]{:S(2)}) async-start(f32[8,16,2048]{2,1,0:T(8,128)} %copy.115), calls=%async_computation.5 | async-start | bytes 2097152 | tf_op jit(solution)/shard_map/all_to_all | solution.py:51
  611.7 26.4 %copy-start.68 = (s32[16]{0:T(128)S(1)}, s32[16]{0:T(128)}, u32[]{:S(2)}) copy-start(s32[16]{0:T(128)} %copy-done.67) | copy-start | bytes 196
  632.1 29.6 %all-to-all-start.9 = ((f32[8,16,2048]{2,1,0:T(8,128)}), f32[8,16,2048]{2,1,0:T(8,128)S(1)}, u32[]{:S(2)}, u32[]{:S(2)}) async-start(f32[8,16,2048]{2,1,0:T(8,128)} %copy.122), calls=%async_computation.9 | async-start | bytes 2097152 | tf_op jit(solution)/shard_map/all_to_all | solution.py:51
  640.3 2.0 copy-start.36
  640.4 2.0 copy-start.62
  640.4 2.0 copy-start.64
  642.4 26.0 %copy-start.3 = (f32[130,2048]{1,0:T(8,128)S(1)}, f32[130,2048]{1,0:T(8,128)}, u32[]{:S(2)}) copy-start(f32[130,2048]{1,0:T(8,128)} %copy-done.2) | copy-start | bytes 3194884
  645.4 22.9 %copy-start.1 = (f32[130,2048]{1,0:T(8,128)S(1)}, f32[130,2048]{1,0:T(8,128)}, u32[]{:S(2)}) copy-start(f32[130,2048]{1,0:T(8,128)} %copy-done) | copy-start | bytes 3194884
  661.6 6.7 copy-start.20
  661.6 81.8 %all-to-all-start.11 = ((bf16[8,16,2048]{2,1,0:T(8,128)(2,1)}), bf16[8,16,2048]{2,1,0:T(8,128)(2,1)}, u32[]{:S(2)}, u32[]{:S(2)}) async-start(bf16[8,16,2048]{2,1,0:T(8,128)(2,1)} %copy.124), calls=%async_computation.11 | async-start | bytes 1048576 | tf_op jit(solution)/shard_map/all_to_all | solution.py:51
  668.1 74.7 %all-reduce.3.cloned.1.call-start = ((), (), s32[]{:S(2)}) async-start(), calls=%async_computation.14 | async-start | bytes 196608 | tf_op jit(solution)/shard_map/psum | solution.py:256
  668.3 4.8 copy-start.61
  668.4 82.6 %copy-start.56 = (f32[1,1,2048]{2,1,0:T(1,128)S(1)}, f32[1,1,2048]{2,1,0:T(1,128)}, u32[]{:S(2)}) copy-start(f32[1,1,2048]{2,1,0:T(1,128)} %copy-done.55) | copy-start | bytes 24580
  668.4 82.6 %copy-start.58 = (f32[1,1,2048]{2,1,0:T(1,128)S(1)}, f32[1,1,2048]{2,1,0:T(1,128)}, u32[]{:S(2)}) copy-start(f32[1,1,2048]{2,1,0:T(1,128)} %copy-done.57) | copy-start | bytes 24580
  668.4 82.6 %copy-start.60 = (f32[1,1,2048]{2,1,0:T(1,128)S(1)}, f32[1,1,2048]{2,1,0:T(1,128)}, u32[]{:S(2)}) copy-start(f32[1,1,2048]{2,1,0:T(1,128)} %copy-done.59) | copy-start | bytes 24580
  672.2 82.2 %copy-start.19 = (f32[128,2048]{1,0:T(8,128)S(1)}, f32[128,2048]{1,0:T(8,128)}, u32[]{:S(2)}) copy-start(f32[128,2048]{1,0:T(8,128)} %get-tuple-element.88) | copy-start | bytes 3145732
  672.2 82.2 %copy-start.44 = (f32[1,1,2048]{2,1,0:T(1,128)S(1)}, f32[1,1,2048]{2,1,0:T(1,128)}, u32[]{:S(2)}) copy-start(f32[1,1,2048]{2,1,0:T(1,128)} %copy-done.43) | copy-start | bytes 24580
  672.2 82.2 %copy-start.46 = (f32[1,1,2048]{2,1,0:T(1,128)S(1)}, f32[1,1,2048]{2,1,0:T(1,128)}, u32[]{:S(2)}) copy-start(f32[1,1,2048]{2,1,0:T(1,128)} %copy-done.45) | copy-start | bytes 24580
  672.2 82.2 %copy-start.48 = (f32[1,1,2048]{2,1,0:T(1,128)S(1)}, f32[1,1,2048]{2,1,0:T(1,128)}, u32[]{:S(2)}) copy-start(f32[1,1,2048]{2,1,0:T(1,128)} %copy-done.47) | copy-start | bytes 24580
  672.2 82.2 %copy-start.50 = (f32[1,1,2048]{2,1,0:T(1,128)S(1)}, f32[1,1,2048]{2,1,0:T(1,128)}, u32[]{:S(2)}) copy-start(f32[1,1,2048]{2,1,0:T(1,128)} %copy-done.49) | copy-start | bytes 24580
  672.3 82.2 %copy-start.52 = (f32[1,1,2048]{2,1,0:T(1,128)S(1)}, f32[1,1,2048]{2,1,0:T(1,128)}, u32[]{:S(2)}) copy-start(f32[1,1,2048]{2,1,0:T(1,128)} %copy-done.51) | copy-start | bytes 24580
  672.3 82.2 %copy-start.54 = (f32[1,1,2048]{2,1,0:T(1,128)S(1)}, f32[1,1,2048]{2,1,0:T(1,128)}, u32[]{:S(2)}) copy-start(f32[1,1,2048]{2,1,0:T(1,128)} %copy-done.53) | copy-start | bytes 24580
  673.0 103.2 %all-reduce.5.cloned.1.call-start = ((), (), s32[]{:S(2)}) async-start(), calls=%async_computation.15 | async-start | bytes 196608 | tf_op jit(solution)/shard_map/psum | solution.py:257
  698.7 52.2 %collective-permute-start.3 = (f32[2,2048]{1,0:T(2,128)S(1)}, f32[2,2048]{1,0:T(2,128)S(1)}, u32[]{:S(2)}, u32[]{:S(2)}) collective-permute-start(f32[2,2048]{1,0:T(2,128)S(1)} %slice.390), channel_id=1, source_target_pairs={{1,0},{2,1},{3,2},{4,3},{5,4},{6,5},{7,6},{9,8},{10,9},{11,10},{12... | collective-permute-start | bytes 49160 | tf_op jit(solution)/shard_map/ppermute | solution.py:10
  742.8 57.7 %reduce-scatter.2.cloned.1.call-start = ((), (), s32[]{:S(2)}) async-start(), calls=%async_computation.13 | async-start | bytes 655360 | tf_op jit(solution)/shard_map/reduce_scatter | solution.py:235
  744.4 10.0 %collective-permute-start.4 = (f32[2,2048]{1,0:T(2,128)S(1)}, f32[2,2048]{1,0:T(2,128)S(1)}, u32[]{:S(2)}, u32[]{:S(2)}) collective-permute-start(f32[2,2048]{1,0:T(2,128)S(1)} %slice.406), channel_id=1, source_target_pairs={{1,0},{2,1},{3,2},{4,3},{5,4},{6,5},{7,6},{9,8},{10,9},{11,10},{12... | collective-permute-start | bytes 49160 | tf_op jit(solution)/shard_map/ppermute | solution.py:10
  747.8 6.6 collective-permute-start.5
  (26 other events, 41.1 us)
Sparse Core Ops, SparseCore 0:
  673.2 69.5 all-reduce.2
  745.1 31.0 all-reduce.4
  778.8 21.6 reduce-scatter.1
